TPU v7x, 128 devices: a whole 4x4x4 slice. The times are simulated.
128 devices in a mesh: grp: 32 (over y, x, core), own: 4 (over z).
Axes of the slice: x: 4, y: 4, z: 4, core: 2. Of those that a mesh axis runs over, the one named last changes fastest.
Arguments:
- background: bfloat16 [256, 1024, 512], P('grp', 'own'), may hold values from -6 to 6
- obs_ens: bfloat16 [256, 2048, 512], P('grp', 'own'), may hold values from -12 to 12
- innovation: bfloat16 [256, 2048], P('grp', 'own'), may hold values from -6 to 6
- obs_weight: bfloat16 [256, 2048], P('grp', 'own'), may hold values from 0.25 to 4
- obs_count: int32 [256, 4], P('grp', 'own'), may hold values from 128 to 512, as said below
- dest: int32 [256], replicated, may hold values from 0 to 31, as said below
Outputs:
- analysis: bfloat16 [256, 1024, 512], P('grp', 'own')
Inputs may be any that keep to these rules, and one draw needn't show every extreme that they name: `obs_count`: each entry counts the live leading slots of one owner's block of 512; later slots carry values that must be ignored. The largest entry of every draw equals 512. `dest`: every index of grp is named by exactly 8 groups, and no two groups of one index of grp name the same index.
All inputs are finite; a program needn't handle non-finite values.
Results may differ from a plain program's by a relative error of at most 0.012.
The roundings to bfloat16 on the way count: a program that leaves them out, or rounds other values in their place, can miss the bound.
Values may be sent and summed in bfloat16 or wider, within the bound.
A program may use at most 128 MiB of HBM per device.

v0:
```python
import jax
import jax.numpy as jnp
from jax import lax
from jax.sharding import PartitionSpec as P

NS_IT = 4


def newton_weights(gram, right_side):
    members = gram.shape[-1]
    eye_mat = jnp.eye(members, dtype=jnp.float32)
    matrix = gram + (members - 1.0) * eye_mat
    norm_scale = jnp.sqrt(jnp.sum(matrix * matrix, axis=(1, 2)))
    root_iter = (matrix / norm_scale[:, None, None]).astype(jnp.bfloat16)
    inverse = jnp.broadcast_to(eye_mat.astype(jnp.bfloat16), matrix.shape)
    for iteration in range(NS_IT):
        product = jnp.einsum("gij,gjk->gik", inverse, root_iter, preferred_element_type=jnp.float32)
        factor = (1.5 * eye_mat - 0.5 * product).astype(jnp.bfloat16)
        root_iter = jnp.einsum(
            "gij,gjk->gik", root_iter, factor, preferred_element_type=jnp.float32
        ).astype(jnp.bfloat16)
        inverse = jnp.einsum(
            "gij,gjk->gik", factor, inverse, preferred_element_type=jnp.float32
        ).astype(jnp.bfloat16)
    inverse_wide = inverse.astype(jnp.float32)
    half_way = jnp.einsum("gij,gj->gi", inverse_wide, right_side)
    mean_weight = jnp.einsum("gij,gj->gi", inverse_wide, half_way) / norm_scale[:, None]
    weights = (
        jnp.sqrt((members - 1.0) / norm_scale)[:, None, None] * inverse_wide
        + mean_weight[:, :, None]
    )
    return weights.astype(jnp.bfloat16)


def solve_weights(obs_pert, weight, source):
    weighted = (obs_pert.astype(jnp.float32) * weight.astype(jnp.float32)[:, :, None]).astype(
        jnp.bfloat16
    )
    gram_local = jnp.einsum("gpk,gpl->gkl", weighted, obs_pert, preferred_element_type=jnp.float32)
    right_local = jnp.einsum("gp,gpk->gk", source, obs_pert, preferred_element_type=jnp.float32)
    gram_part, right_part = (
        lax.psum_scatter(gram_local, "own", scatter_dimension=0, tiled=True),
        lax.psum_scatter(right_local, "own", scatter_dimension=0, tiled=True),
    )
    return lax.all_gather(newton_weights(gram_part, right_part), "own", axis=0, tiled=True)


def apply_weights(state_here, weights):
    state_mean = jnp.mean(state_here.astype(jnp.float32), axis=2, keepdims=True)
    state_pert = (state_here.astype(jnp.float32) - state_mean).astype(jnp.bfloat16)
    result = state_mean + jnp.einsum(
        "grk,gkl->grl", state_pert, weights, preferred_element_type=jnp.float32
    )
    return result.astype(jnp.bfloat16)


def pack_rows(array_in, send_index, send_live):
    picked = jnp.take(array_in, send_index, axis=0)
    keep_mask = send_live.reshape((-1,) + (1,) * (array_in.ndim - 1))
    return jnp.where(keep_mask, picked, jnp.zeros_like(picked))


def body(background, obs_ens, innovation, obs_weight, obs_count, dest):
    grp_size = lax.axis_size("grp")
    grp_index = lax.axis_index("grp")
    local_groups = background.shape[0]
    obs_rows = obs_ens.shape[1]
    obs_mean = jnp.mean(obs_ens.astype(jnp.float32), axis=2, keepdims=True)
    obs_pert = (obs_ens.astype(jnp.float32) - obs_mean).astype(jnp.bfloat16)
    position_in = lax.broadcasted_iota(jnp.int32, (local_groups, obs_rows), 1)
    live_rows = position_in < obs_count
    weight = jnp.where(live_rows, obs_weight, jnp.zeros_like(obs_weight))
    source = (weight.astype(jnp.float32) * innovation.astype(jnp.float32)).astype(jnp.bfloat16)
    group_total = dest.shape[0]
    group_ids = jnp.arange(group_total, dtype=jnp.int32)
    same_dest = dest[None, :] == dest[:, None]
    earlier = group_ids[None, :] < group_ids[:, None]
    arrival_rank = jnp.sum(jnp.where(same_dest & earlier, 1, 0), axis=1).astype(jnp.int32)
    my_dest = lax.dynamic_slice_in_dim(dest, grp_index * local_groups, local_groups)
    peer_ids = jnp.arange(grp_size, dtype=jnp.int32)
    local_ids = jnp.arange(local_groups, dtype=jnp.int32)
    peer_hits = my_dest[None, :] == peer_ids[:, None]
    send_index = jnp.sum(jnp.where(peer_hits, local_ids[None, :], 0), axis=1)
    send_live = jnp.any(peer_hits, axis=1)
    arriving = (dest[None, :] == grp_index) & (arrival_rank[None, :] == local_ids[:, None])
    arrive_group = jnp.sum(jnp.where(arriving, group_ids[None, :], 0), axis=1)
    arrive_source = arrive_group // local_groups
    weights = solve_weights(obs_pert, weight, source)
    result = apply_weights(background, weights)
    return jnp.take(
        lax.all_to_all(
            pack_rows(result, send_index, send_live), "grp", split_axis=0, concat_axis=0, tiled=True
        ),
        arrive_source,
        axis=0,
    )


def solution(mesh):
    return jax.shard_map(
        body,
        mesh=mesh,
        in_specs=(
            P("grp", "own", None),
            P("grp", "own", None),
            P("grp", "own"),
            P("grp", "own"),
            P("grp", "own"),
            P(),
        ),
        out_specs=P("grp", "own", None),
        check_vma=False,
    )
```

profile of v0, /device:TPU:1, one launch (start us, length us, event | category | flops | bytes accessed | tf_op | source)
XLA Modules:
  0.0 304.8 jit_solution(16136951597792057878)
XLA Ops:
  6.5 3.0 convert_reduce_fusion
  9.6 0.4 copy-done
  10.0 6.3 %fusion.1 = f32[8,512,512]{2,1,0:T(8,128)} fusion(f32[8,512]{1,0:T(8,128)S(1)} %fusion.16, bf16[8,512,512]{2,1,0:T(8,128)(2,1)S(1)} %copy-done, f32[8,512]{1,0:T(8,128)S(1)} %broadcast_multiply_fusion), kind=kOutput, calls=%fused_computation.7 | convolution fusion | flops 2166358016 | bytes 12615680 | tf_op jit(solution)/shard_map/gpk,gpl->gkl/dot_general | solution.py:39
  16.4 0.6 copy-done.5
  17.1 2.8 fusion.5
  19.9 0.6 dynamic-slice
  21.1 16.5 %all-reduce = bf16[8,512]{1,0:T(8,128)(2,1)S(1)} all-reduce(f32[8,512]{1,0:T(8,128)S(1)} %bitcast.53), channel_id=3, replica_groups=mesh['grp'=32,'own'=4] {'own'}, use_global_device_ids=true, to_apply=%region_8.9.clone | all-reduce | flops 4096 | bytes 24576
  37.9 62.8 %reduce-scatter.2.cloned.1.call-done = f32[2,512,512]{2,1,0:T(8,128)} async-done(((f32[8,512,512]{2,1,0:T(8,128)}), f32[2,512,512]{2,1,0:T(8,128)}) %reduce-scatter.2.cloned.1.call-update) | async-done | bytes 2097168 | tf_op jit(solution)/shard_map/reduce_scatter | solution.py:42
  100.7 2.1 multiply_reduce_fusion
  102.9 0.6 divide_convert_fusion
  103.5 0.7 subtract_convert_fusion.3
  104.2 0.7 convolution_convert_fusion.5
  104.9 0.7 convolution_convert_fusion.6
  105.6 0.7 subtract_convert_fusion.2
  106.4 0.7 convolution_convert_fusion.3
  107.1 0.7 convolution_convert_fusion.4
  107.8 0.7 subtract_convert_fusion.1
  108.6 1.0 copy-done.8
  109.5 1.7 convolution_convert_fusion.2
  111.2 3.8 %subtract_convert_fusion = bf16[2,512,512]{2,1,0:T(8,128)(2,1)} fusion(bf16[2,512,512]{2,1,0:T(8,128)(2,1)} %convolution_convert_fusion.2, bf16[2,512,512]{2,1,0:T(8,128)(2,1)S(1)} %convolution_convert_fusion.3, bf16[2,512,512]{2,1,0:T(8,128)(2,1)} %copy-done.8, f32[512,512]{1,0:T(8,128)S(1)} %fusion.9), kind=kOutput, calls=%fused_computation.15 | convolution fusion | flops 1075838976 | bytes 5242880 | tf_op jit(solution)/shard_map/gij,gjk->gik/dot_general | solution.py:17
  115.0 2.2 convolution_convert_fusion
  117.3 0.4 fusion.21
  117.7 0.4 fusion.19
  118.1 1.3 add_convert_fusion.1
  120.1 47.2 %all-gather.2.cloned.1.call-done = bf16[8,512,512]{2,1,0:T(8,128)(2,1)} async-done(((bf16[2,512,512]{2,1,0:T(8,128)(2,1)}), bf16[8,512,512]{2,1,0:T(8,128)(2,1)}) %all-gather.2.cloned.1.call-update) | async-done | bytes 4194320 | tf_op jit(solution)/shard_map/all_gather | solution.py:45
  167.3 4.1 %add_convert_fusion = bf16[8,256,512]{2,1,0:T(8,128)(2,1)S(1)} fusion(bf16[8,512,512]{2,1,0:T(8,128)(2,1)} %all-gather.2.cloned.1.call-done, bf16[8,256,512]{2,1,0:T(8,128)(2,1)} %param.6, f32[8,256]{1,0:T(8,128)S(1)} %broadcast_multiply_fusion.1), kind=kOutput, calls=%fused_computation.11 | convolution fusion | flops 1078984704 | bytes 8396800 | tf_op jit(solution)/shard_map/grk,gkl->grl/dot_general | solution.py:51
  171.5 4.8 %gather_fusion = bf16[32,256,512]{2,1,0:T(8,128)(2,1)} fusion(bf16[8,256,512]{2,1,0:T(8,128)(2,1)S(1)} %add_convert_fusion, s32[1024]{0:T(1024)S(1)} %pad_clamp_fusion.1), kind=kCustom, calls=%fused_computation | custom fusion | bytes 16777344 | tf_op jit(solution)/shard_map/jit(_take)/gather | solution.py:58
  176.3 7.6 %select_select_fusion = bf16[32,256,512]{2,1,0:T(8,128)(2,1)} fusion(bf16[32,256,512]{2,1,0:T(8,128)(2,1)} %gather_fusion, pred[32]{0:T(512)(128)(4,1)S(1)} %compare_and_fusion, pred[32]{0:T(512)(128)(4,1)S(1)} %fusion.23), kind=kLoop, calls=%fused_computation.5 | loop fusion | flops 8388608 | bytes 16777280 | tf_op jit(solution)/shard_map/jit(_where)/select_n | solution.py:60
  183.9 7.8 %all-to-all-start = ((bf16[32,256,512]{2,1,0:T(8,128)(2,1)}), bf16[32,256,512]{2,1,0:T(8,128)(2,1)}, u32[]{:S(2)}, u32[]{:S(2)}) async-start(bf16[32,256,512]{2,1,0:T(8,128)(2,1)} %select_select_fusion), calls=%async_computation.1 | async-start | bytes 16777216 | tf_op jit(solution)/shard_map/all_to_all | solution.py:91
  192.0 100.3 %all-to-all-done = bf16[32,256,512]{2,1,0:T(8,128)(2,1)} async-done(((bf16[32,256,512]{2,1,0:T(8,128)(2,1)}), bf16[32,256,512]{2,1,0:T(8,128)(2,1)}, u32[]{:S(2)}, u32[]{:S(2)}) %all-to-all-start) | async-done | bytes 8388640 | tf_op jit(solution)/shard_map/all_to_all | solution.py:91
  292.3 4.1 %gather_fusion.1 = bf16[8,256,512]{2,1,0:T(8,128)(2,1)S(1)} fusion(bf16[32,256,512]{2,1,0:T(8,128)(2,1)} %all-to-all-done, s32[1024]{0:T(1024)S(1)} %pad_clamp_fusion), kind=kCustom, calls=%fused_computation.1 | custom fusion | bytes 4194336 | tf_op jit(solution)/shard_map/jit(_take)/gather | solution.py:90
  296.4 1.6 broadcast_select_fusion
  (44 shorter events, 1.7 us)
Async XLA Ops:
  6.5 3.0 copy-start.6
  6.5 3.0 copy-start.3
  6.5 94.1 %reduce-scatter.2.cloned.1.call-start = ((), (), s32[]{:S(2)}) async-start(), calls=%async_computation.2 | async-start | bytes 10485760 | tf_op jit(solution)/shard_map/reduce_scatter | solution.py:42
  6.5 3.5 %copy-start = (bf16[8,512,512]{2,1,0:T(8,128)(2,1)S(1)}, bf16[8,512,512]{2,1,0:T(8,128)(2,1)}, u32[]{:S(2)}) copy-start(bf16[8,512,512]{2,1,0:T(8,128)(2,1)} %param.7) | copy-start | bytes 12582916
  16.3 0.7 copy-start.5
  16.3 151.0 %all-gather.2.cloned.1.call-start = ((), (), s32[]{:S(2)}) async-start(), calls=%async_computation.3 | async-start | bytes 5242880 | tf_op jit(solution)/shard_map/all_gather | solution.py:45
  17.1 2.8 copy-start.7
  100.7 2.2 copy-start.1
  108.5 1.0 copy-start.8
  117.7 1.8 copy-start.4
  117.7 2.1 copy-start.2
  183.9 108.5 %all-to-all-start = ((bf16[32,256,512]{2,1,0:T(8,128)(2,1)}), bf16[32,256,512]{2,1,0:T(8,128)(2,1)}, u32[]{:S(2)}, u32[]{:S(2)}) async-start(bf16[32,256,512]{2,1,0:T(8,128)(2,1)} %select_select_fusion), calls=%async_computation.1 | async-start | bytes 16777216 | tf_op jit(solution)/shard_map/all_to_all | solution.py:91
Sparse Core Ops, SparseCore 0:
  16.4 84.1 reduce-scatter.1
  119.6 47.6 all-gather.1
where the time goes:
time: 309 us; the launch traced here: 305 us
  waiting for transfers between devices  210 us (68%)
  matrix products  26.7 us (9%)
  other arithmetic  17.5 us (6%)
  blocking collectives  16.5 us (5%)
  between operations  14.3 us (5%)
  local copies, waits for them, and re-layouts  11.7 us (4%)
  starting transfers between devices  7.8 us (3%)
    all_to_all x1, waiting for transfers between devices, body(): lax.all_to_all(pack_rows(result, send_index, send_live), 'grp', split_axi...  100 us
    reduce_scatter x1, waiting for transfers between devices, solve_weights(): lax.psum_scatter(gram_local, 'own', scatter_dimension=0, tiled=True)  62.8 us
    all_gather x1, waiting for transfers between devices, solve_weights(): lax.all_gather(newton_weights(gram_part, right_part), 'own', axis=0, tile...  47.2 us
    unnamed x1, blocking collectives  16.5 us
    all_to_all x1, starting transfers between devices, body(): lax.all_to_all(pack_rows(result, send_index, send_live), 'grp', split_axi...  7.75 us
    select_n x1, other arithmetic, pack_rows(): return jnp.where(keep_mask, picked, jnp.zeros_like(picked))  7.57 us
    dot_general x1, matrix products, solve_weights(): jnp.einsum('gpk,gpl->gkl', weighted, obs_pert, preferred_element_type=jnp...  6.28 us
  transfers between devices with their start and end apart: 3, of which 3 were waited for; matrix products, arithmetic and copies ran while one was open for 2% of the time, Pallas kernels for 0%

commit v1 on v0

--- a/solution.py
+++ b/solution.py
@@ -54,15 +54,28 @@
     return result.astype(jnp.bfloat16)
 
 
-def pack_rows(array_in, send_index, send_live):
-    picked = jnp.take(array_in, send_index, axis=0)
-    keep_mask = send_live.reshape((-1,) + (1,) * (array_in.ndim - 1))
-    return jnp.where(keep_mask, picked, jnp.zeros_like(picked))
+def route(result, dest):
+    grp_size = lax.axis_size("grp")
+    local_groups, rows, members = result.shape
+    group_total = dest.shape[0]
+    group_ids = jnp.arange(group_total, dtype=jnp.int32)
+    same_dest = dest[None, :] == dest[:, None]
+    earlier = group_ids[None, :] < group_ids[:, None]
+    arrival_rank = jnp.sum(jnp.where(same_dest & earlier, 1, 0), axis=1).astype(jnp.int32)
+    slot_of = dest * local_groups + arrival_rank
+    holder = jnp.sum(
+        jnp.where(slot_of[None, :] == group_ids[:, None], group_ids[None, :], 0), axis=1
+    ).astype(jnp.int32)
+    piece = rows // grp_size
+    pieces = result.reshape(local_groups, grp_size, piece, members).swapaxes(0, 1)
+    spread = lax.all_to_all(pieces, "grp", split_axis=0, concat_axis=0, tiled=True)
+    spread = spread.reshape(group_total, piece, members)
+    ordered = jnp.take(spread, holder, axis=0).reshape(grp_size, local_groups, piece, members)
+    back = lax.all_to_all(ordered, "grp", split_axis=0, concat_axis=0, tiled=True)
+    return back.swapaxes(0, 1).reshape(local_groups, rows, members)
 
 
 def body(background, obs_ens, innovation, obs_weight, obs_count, dest):
-    grp_size = lax.axis_size("grp")
-    grp_index = lax.axis_index("grp")
     local_groups = background.shape[0]
     obs_rows = obs_ens.shape[1]
     obs_mean = jnp.mean(obs_ens.astype(jnp.float32), axis=2, keepdims=True)
@@ -71,29 +84,9 @@
     live_rows = position_in < obs_count
     weight = jnp.where(live_rows, obs_weight, jnp.zeros_like(obs_weight))
     source = (weight.astype(jnp.float32) * innovation.astype(jnp.float32)).astype(jnp.bfloat16)
-    group_total = dest.shape[0]
-    group_ids = jnp.arange(group_total, dtype=jnp.int32)
-    same_dest = dest[None, :] == dest[:, None]
-    earlier = group_ids[None, :] < group_ids[:, None]
-    arrival_rank = jnp.sum(jnp.where(same_dest & earlier, 1, 0), axis=1).astype(jnp.int32)
-    my_dest = lax.dynamic_slice_in_dim(dest, grp_index * local_groups, local_groups)
-    peer_ids = jnp.arange(grp_size, dtype=jnp.int32)
-    local_ids = jnp.arange(local_groups, dtype=jnp.int32)
-    peer_hits = my_dest[None, :] == peer_ids[:, None]
-    send_index = jnp.sum(jnp.where(peer_hits, local_ids[None, :], 0), axis=1)
-    send_live = jnp.any(peer_hits, axis=1)
-    arriving = (dest[None, :] == grp_index) & (arrival_rank[None, :] == local_ids[:, None])
-    arrive_group = jnp.sum(jnp.where(arriving, group_ids[None, :], 0), axis=1)
-    arrive_source = arrive_group // local_groups
     weights = solve_weights(obs_pert, weight, source)
     result = apply_weights(background, weights)
-    return jnp.take(
-        lax.all_to_all(
-            pack_rows(result, send_index, send_live), "grp", split_axis=0, concat_axis=0, tiled=True
-        ),
-        arrive_source,
-        axis=0,
-    )
+    return route(result, dest)
 
 
 def solution(mesh):

time: 309 us -> 255 us (0.83); the launches traced: 305 us -> 254 us
  waiting for transfers between devices: 210 us -> 138 us
  blocking collectives: 16.5 us -> 49.3 us
  other arithmetic: 17.5 us -> 8.6 us
    all_to_all x1, waiting for transfers between devices: 100 us -> 28.1 us  [route(): lax.all_to_all(pieces, 'grp', split_axis=0, concat_axis=0, tiled=True)]
    all_to_all x0 -> x1, blocking collectives: none -> 32.8 us  [route(): lax.all_to_all(ordered, 'grp', split_axis=0, concat_axis=0, tiled=True)]
    select_n x4 -> x2, other arithmetic: 9.17 us -> 0.46 us  [route(): jnp.take(spread, holder, axis=0)]
    gather x2 -> x1, local copies, waits for them, and re-layouts: 8.9 us -> 2.34 us  [route(): jnp.take(spread, holder, axis=0)]
where the time goes in v1:
time: 255 us; the launch traced here: 254 us
  waiting for transfers between devices  138 us (54%)
  blocking collectives  49.3 us (19%)
  matrix products  26.3 us (10%)
  between operations  14.3 us (6%)
  local copies, waits for them, and re-layouts  9.52 us (4%)
  other arithmetic  8.6 us (3%)
  starting transfers between devices  7.87 us (3%)
    reduce_scatter x1, waiting for transfers between devices, solve_weights(): lax.psum_scatter(gram_local, 'own', scatter_dimension=0, tiled=True)  62.8 us
    all_gather x1, waiting for transfers between devices, solve_weights(): lax.all_gather(newton_weights(gram_part, right_part), 'own', axis=0, tile...  47.5 us
    all_to_all x1, blocking collectives, route(): lax.all_to_all(ordered, 'grp', split_axis=0, concat_axis=0, tiled=True)  32.8 us
    all_to_all x1, waiting for transfers between devices, route(): lax.all_to_all(pieces, 'grp', split_axis=0, concat_axis=0, tiled=True)  28.1 us
    unnamed x1, blocking collectives  16.5 us
    all_to_all x1, starting transfers between devices, route(): lax.all_to_all(pieces, 'grp', split_axis=0, concat_axis=0, tiled=True)  7.83 us
    dot_general x1, matrix products, solve_weights(): jnp.einsum('gpk,gpl->gkl', weighted, obs_pert, preferred_element_type=jnp...  6.28 us
    dot_general x4, matrix products, newton_weights(): jnp.einsum('gij,gjk->gik', inverse, root_iter, preferred_element_type=jnp...  6.01 us
  transfers between devices with their start and end apart: 3, of which 3 were waited for; matrix products, arithmetic and copies ran while one was open for 2% of the time, Pallas kernels for 0%

profile of v1, /device:TPU:1, one launch (start us, length us, event | category | flops | bytes accessed | tf_op | source)
XLA Modules:
  0.0 254.3 jit_solution(15202056661107613254)
XLA Ops:
  6.5 3.0 %convert_reduce_fusion = f32[8,512]{1,0:T(8,128)S(1)} fusion(bf16[8,512,512]{2,1,0:T(8,128)(2,1)} %param.7), kind=kLoop, calls=%fused_computation.2 | loop fusion | flops 4190208 | bytes 4210688 | tf_op jit(solution)/shard_map/reduce_sum | solution.py:81
  9.6 0.4 copy-done
  10.0 6.3 %fusion.1 = f32[8,512,512]{2,1,0:T(8,128)} fusion(f32[8,512]{1,0:T(8,128)S(1)} %fusion.19, bf16[8,512,512]{2,1,0:T(8,128)(2,1)S(1)} %copy-done, f32[8,512]{1,0:T(8,128)S(1)} %broadcast_multiply_fusion), kind=kOutput, calls=%fused_computation.5 | convolution fusion | flops 2166358016 | bytes 12615680 | tf_op jit(solution)/shard_map/gpk,gpl->gkl/dot_general | solution.py:39
  16.4 0.6 copy-done.6
  17.1 2.8 %fusion.5 = f32[8,1,512]{2,1,0:T(1,128)S(1)} fusion(bf16[8,512,512]{2,1,0:T(8,128)(2,1)} %param.7, f32[8,512]{1,0:T(8,128)S(1)} %broadcast_multiply_fusion, bf16[8,512,1]{1,0,2:T(8,128)(2,1)S(1)} %fusion.20), kind=kOutput, calls=%fused_computation.11 | convolution fusion | flops 10485760 | bytes 4235264 | tf_op jit(solution)/shard_map/gp,gpk->gk/dot_general | solution.py:40
  19.9 0.6 dynamic-slice
  21.1 16.5 %all-reduce = bf16[8,512]{1,0:T(8,128)(2,1)S(1)} all-reduce(f32[8,512]{1,0:T(8,128)S(1)} %bitcast.54), channel_id=3, replica_groups=mesh['grp'=32,'own'=4] {'own'}, use_global_device_ids=true, to_apply=%region_6.7.clone | all-reduce | flops 4096 | bytes 24576
  37.9 62.8 %reduce-scatter.2.cloned.1.call-done = f32[2,512,512]{2,1,0:T(8,128)} async-done(((f32[8,512,512]{2,1,0:T(8,128)}), f32[2,512,512]{2,1,0:T(8,128)}) %reduce-scatter.2.cloned.1.call-update) | async-done | bytes 2097168 | tf_op jit(solution)/shard_map/reduce_scatter | solution.py:42
  100.7 2.1 multiply_reduce_fusion
  102.9 0.6 divide_convert_fusion
  103.5 0.7 subtract_convert_fusion.3
  104.2 0.7 convolution_convert_fusion.5
  104.9 0.7 convolution_convert_fusion.6
  105.6 0.7 subtract_convert_fusion.2
  106.4 0.7 convolution_convert_fusion.3
  107.1 0.7 convolution_convert_fusion.4
  107.8 0.7 subtract_convert_fusion.1
  108.6 1.0 copy-done.9
  109.5 1.7 convolution_convert_fusion.2
  111.2 3.8 %subtract_convert_fusion = bf16[2,512,512]{2,1,0:T(8,128)(2,1)} fusion(bf16[2,512,512]{2,1,0:T(8,128)(2,1)} %convolution_convert_fusion.2, bf16[2,512,512]{2,1,0:T(8,128)(2,1)S(1)} %convolution_convert_fusion.3, bf16[2,512,512]{2,1,0:T(8,128)(2,1)} %copy-done.9, f32[512,512]{1,0:T(8,128)S(1)} %fusion.12), kind=kOutput, calls=%fused_computation.15 | convolution fusion | flops 1075838976 | bytes 5242880 | tf_op jit(solution)/shard_map/gij,gjk->gik/dot_general | solution.py:17
  115.1 2.2 convolution_convert_fusion
  118.1 1.3 add_convert_fusion.1
  119.8 47.5 %all-gather.2.cloned.1.call-done = bf16[8,512,512]{2,1,0:T(8,128)(2,1)} async-done(((bf16[2,512,512]{2,1,0:T(8,128)(2,1)}), bf16[8,512,512]{2,1,0:T(8,128)(2,1)}) %all-gather.2.cloned.1.call-update) | async-done | bytes 4194320 | tf_op jit(solution)/shard_map/all_gather | solution.py:45
  167.3 3.7 %fusion.9 = bf16[8,32,8,512]{3,2,1,0:T(8,128)(2,1)S(1)} fusion(bf16[8,512,512]{2,1,0:T(8,128)(2,1)} %all-gather.2.cloned.1.call-done, bf16[8,256,512]{2,1,0:T(8,128)(2,1)S(1)} %copy-done.3, f32[8,256]{1,0:T(8,128)S(1)} %broadcast_multiply_fusion.1), kind=kOutput, calls=%fused_computation.23 | convolution fusion | flops 1078984704 | bytes 8396800 | tf_op jit(solution)/shard_map/grk,gkl->grl/dot_general | solution.py:51
  171.0 1.6 copy.37
  172.6 7.8 %all-to-all-start = ((bf16[32,8,8,512]{3,2,1,0:T(8,128)(2,1)}), bf16[32,8,8,512]{3,2,1,0:T(8,128)(2,1)S(1)}, u32[]{:S(2)}, u32[]{:S(2)}) async-start(bf16[32,8,8,512]{3,2,1,0:T(8,128)(2,1)} %bitcast.53), calls=%async_computation.1 | async-start | bytes 4194304 | tf_op jit(solution)/shard_map/all_to_all | solution.py:71
  180.9 28.1 %all-to-all-done = bf16[32,8,8,512]{3,2,1,0:T(8,128)(2,1)S(1)} async-done(((bf16[32,8,8,512]{3,2,1,0:T(8,128)(2,1)}), bf16[32,8,8,512]{3,2,1,0:T(8,128)(2,1)S(1)}, u32[]{:S(2)}, u32[]{:S(2)}) %all-to-all-start) | async-done | bytes 2097184 | tf_op jit(solution)/shard_map/all_to_all | solution.py:71
  209.0 1.3 copy-done.1
  210.4 2.3 gather_fusion
  212.7 0.5 broadcast_select_fusion
  213.2 32.8 %all_to_all.10 = bf16[32,8,8,512]{3,2,1,0:T(8,128)(2,1)S(1)} all-to-all(bf16[32,8,8,512]{3,2,1,0:T(8,128)(2,1)S(1)} %broadcast_select_fusion), channel_id=1, replica_groups=mesh['grp'=32,'own'=4] {'grp'}, dimensions={0} | all-to-all | bytes 4194304 | tf_op jit(solution)/shard_map/all_to_all | solution.py:74
  246.0 1.5 copy_bitcast_fusion
  (42 shorter events, 2.2 us)
Async XLA Ops:
  6.5 3.0 %copy-start.7 = (s32[8,1]{0,1:T(1,128)S(1)}, s32[8,1]{0,1:T(1,128)}, u32[]{:S(2)}) copy-start(s32[8,1]{0,1:T(1,128)} %param.10) | copy-start | bytes 100
  6.5 3.0 %copy-start.4 = (bf16[8,512]{1,0:T(8,128)(2,1)S(1)}, bf16[8,512]{1,0:T(8,128)(2,1)}, u32[]{:S(2)}) copy-start(bf16[8,512]{1,0:T(8,128)(2,1)} %param.9) | copy-start | bytes 24580
  6.5 94.1 %reduce-scatter.2.cloned.1.call-start = ((), (), s32[]{:S(2)}) async-start(), calls=%async_computation.3 | async-start | bytes 10485760 | tf_op jit(solution)/shard_map/reduce_scatter | solution.py:42
  6.5 3.5 %copy-start = (bf16[8,512,512]{2,1,0:T(8,128)(2,1)S(1)}, bf16[8,512,512]{2,1,0:T(8,128)(2,1)}, u32[]{:S(2)}) copy-start(bf16[8,512,512]{2,1,0:T(8,128)(2,1)} %param.7) | copy-start | bytes 12582916
  16.3 0.7 copy-start.6
  16.3 151.0 %all-gather.2.cloned.1.call-start = ((), (), s32[]{:S(2)}) async-start(), calls=%async_computation.4 | async-start | bytes 5242880 | tf_op jit(solution)/shard_map/all_gather | solution.py:45
  17.1 2.8 %copy-start.8 = (u32[128]{0:T(128)S(1)}, u32[128]{0:T(128)}, u32[]{:S(2)}) copy-start(u32[128]{0:T(128)} %constant.46) | copy-start | bytes 1540
  100.7 2.2 copy-start.2
  108.5 1.0 copy-start.9
  117.7 1.8 copy-start.3
  172.6 7.8 %copy-start.5 = (s32[256]{0:T(256)S(1)}, s32[256]{0:T(256)}, u32[]{:S(2)}) copy-start(s32[256]{0:T(256)} %param.11) | copy-start | bytes 3076
  172.6 36.4 %all-to-all-start = ((bf16[32,8,8,512]{3,2,1,0:T(8,128)(2,1)}), bf16[32,8,8,512]{3,2,1,0:T(8,128)(2,1)S(1)}, u32[]{:S(2)}, u32[]{:S(2)}) async-start(bf16[32,8,8,512]{3,2,1,0:T(8,128)(2,1)} %bitcast.53), calls=%async_computation.1 | async-start | bytes 4194304 | tf_op jit(solution)/shard_map/all_to_all | solution.py:71
  209.0 1.3 copy-start.1
Sparse Core Ops, SparseCore 0:
  16.4 84.1 reduce-scatter.1
  119.6 47.6 all-gather.1

commit v2 on v1

v2 whole, which is shorter than its diff:
```python
import random

import jax
import jax.numpy as jnp
from jax import lax
from jax.experimental import pallas as pl
from jax.experimental.pallas import tpu as pltpu
from jax.sharding import PartitionSpec as P

MESH = pl.DeviceIdType.MESH
F32 = jnp.float32
BF16 = jnp.bfloat16
MEMBERS = 512
HALF = 256
GROUPS_HERE = 8
ROUNDS = 2
GRP = 32

ORDER = list(range(1, GRP))
random.Random(23).shuffle(ORDER)


def dot(a, b):
    return jnp.dot(a, b, preferred_element_type=F32)


def dot_nt(a, b):
    return lax.dot_general(a, b, (((1,), (1,)), ((), ())), preferred_element_type=F32)


def eye(n):
    rows = lax.broadcasted_iota(jnp.int32, (n, n), 0)
    cols = lax.broadcasted_iota(jnp.int32, (n, n), 1)
    return jnp.where(rows == cols, 1.0, 0.0).astype(F32)


def kernel(
    holder, obs_hbm, bg_hbm, innov, obs_weight, count, out,
    obs, bg, wrow, src, part, own_part, relay_own, relay_in, owner_in, rhs_part, rhs_in,
    root, inv, fac, vbuf, mwbuf, pert, mean, spread, gathered, picked,
    obs_sem, bg_sem, send_z, recv_z, send_g, recv_g, self_sem,
):
    me = lax.axis_index("grp")
    z = lax.axis_index("own")
    y, x, c = me // 8, lax.rem(me // 2, 4), lax.rem(me, 2)

    def peer(s):
        return (
            lax.rem(y + s // 8, 4) * 8 + lax.rem(x + (s // 2) % 4, 4) * 2 + lax.rem(c + s % 2, 2)
        )

    def zpeer(q):
        return lax.rem(z + q, 4)

    def group(r, q):
        return zpeer(q) * ROUNDS + r

    barrier = pltpu.get_barrier_semaphore()
    for s in ORDER:
        pl.semaphore_signal(barrier, inc=1, device_id={"grp": peer(s)}, device_id_type=MESH)
    for q in (1, 2, 3):
        pl.semaphore_signal(barrier, inc=1, device_id={"own": zpeer(q)}, device_id_type=MESH)

    loads = []
    for r in range(ROUNDS):
        for q in (2, 1, 3, 0):
            load = pltpu.make_async_copy(
                obs_hbm.at[group(r, q)], obs.at[group(r, q)], obs_sem.at[r, q]
            )
            load.start()
            loads.append(load)
    bg_load = pltpu.make_async_copy(bg_hbm, bg, bg_sem)
    bg_load.start()

    position = lax.broadcasted_iota(jnp.int32, (GROUPS_HERE, 512), 1)
    weight = jnp.where(position < count[...], obs_weight[...].astype(F32), 0.0)
    source = (weight * innov[...].astype(F32)).astype(BF16)
    for g in range(GROUPS_HERE):
        wrow[g] = jnp.broadcast_to(weight[g : g + 1], (8, 512))
        src[g] = jnp.broadcast_to(source[g : g + 1].astype(F32), (16, 512)).astype(BF16)

    pending = []

    def zcopy(source_ref, target_ref, q, r, index):
        copy = pltpu.make_async_remote_copy(
            src_ref=source_ref,
            dst_ref=target_ref,
            send_sem=send_z.at[r, index],
            recv_sem=recv_z.at[r, index],
            device_id={"own": zpeer(q)},
            device_id_type=MESH,
        )
        copy.start()
        pending.append(copy)
        return copy

    def gram(r, q):
        g = group(r, q)
        ens = obs[g].astype(F32)
        centred = (ens - jnp.mean(ens, axis=1, keepdims=True)).astype(BF16)
        turned = (centred.astype(F32).T * wrow[g][0:1]).astype(BF16)
        upper = dot(turned[:HALF], centred)
        corner = dot(turned[HALF:], centred[:, HALF:])
        right = dot(src[g], centred)[0:8]
        return (upper[:, :HALF], upper[:, HALF:], corner), right

    relay = {}
    direct = {}
    for r in range(ROUNDS):
        for n, q in enumerate((2, 1, 3, 0)):
            loads[r * 4 + n].wait()
            blocks, right = gram(r, q)
            if r == 0 and n == 0:
                pl.semaphore_wait(barrier, GRP - 1 + 3)
            if q == 0:
                for b in range(3):
                    own_part[r, b] = blocks[b]
                rhs_part[r, 0] = right
                continue
            for b in range(3):
                for h in range(2):
                    piece = blocks[b][h * 128 : (h + 1) * 128]
                    if (q, h) in ((1, 0), (3, 1)):
                        relay_own[r, h, b] = piece
                    else:
                        part[r, q, h, b] = piece.astype(BF16)
            rhs_part[r, q] = right
            if q == 2:
                relay[r, 0] = zcopy(part.at[r, 2, 0], relay_in.at[r, 0], 1, r, 0)
                relay[r, 1] = zcopy(part.at[r, 2, 1], relay_in.at[r, 1], 3, r, 1)
            elif q == 1:
                direct[r, 1] = zcopy(part.at[r, 1, 1], owner_in.at[r, 0, 1], 1, r, 2)
            else:
                direct[r, 0] = zcopy(part.at[r, 3, 0], owner_in.at[r, 1, 0], 3, r, 3)
            direct[r, 1 + q] = zcopy(rhs_part.at[r, q], rhs_in.at[r, q], q, r, 3 + q)
        if r == 0:
            continue
    combined = {}
    for r in range(ROUNDS):
        for h, q in ((0, 1), (1, 3)):
            relay[r, h].wait_recv()
            for b in range(3):
                part[r, q, h, b] = (relay_own[r, h, b] + relay_in[r, h, b].astype(F32)).astype(BF16)
            combined[r, h] = zcopy(
                part.at[r, q, h], owner_in.at[r, 0 if q == 1 else 1, h], q, r, 7 + h
            )

    bg_load.wait()
    for g in range(GROUPS_HERE):
        state = bg[g].astype(F32)
        centre = jnp.mean(state, axis=1, keepdims=True)
        pert[g] = (state - centre).astype(BF16)
        mean[g] = jnp.broadcast_to(centre, (256, 128))

    def sym_rows(rows, blocks):
        high = rows.astype(BF16)
        low = (rows - high.astype(F32)).astype(BF16)
        both = jnp.concatenate([high, low], axis=0)
        a, b = both[:, :HALF], both[:, HALF:]
        left = dot(a, blocks[0]) + dot_nt(b, blocks[1])
        right = dot(a, blocks[1]) + dot(b, blocks[2])
        full = jnp.concatenate([left, right], axis=1)
        return full[0:16] + full[16:32]

    gathers = {}
    for r in range(ROUNDS):
        for h in range(2):
            direct[r, h].wait_recv()
            combined[r, h].wait_recv()
        for q in (1, 2, 3):
            direct[r, 1 + q].wait_recv()
        blocks = []
        for b in range(3):
            total = own_part[r, b]
            total = total + owner_in[r, 0, :, b].astype(F32).reshape(HALF, HALF)
            total = total + owner_in[r, 1, :, b].astype(F32).reshape(HALF, HALF)
            if b != 1:
                total = total + (MEMBERS - 1.0) * eye(HALF)
            blocks.append(total)
        squares = (
            jnp.sum(blocks[0] * blocks[0])
            + 2.0 * jnp.sum(blocks[1] * blocks[1])
            + jnp.sum(blocks[2] * blocks[2])
        )
        scale = jnp.sqrt(jnp.full((1, 1), squares, F32))
        per = 1.0 / scale
        cross = blocks[1] * per
        root[:HALF, :HALF] = (blocks[0] * per).astype(BF16)
        root[:HALF, HALF:] = cross.astype(BF16)
        root[HALF:, :HALF] = cross.T.astype(BF16)
        root[HALF:, HALF:] = (blocks[2] * per).astype(BF16)
        unit = eye(MEMBERS)
        fac[...] = (1.5 * unit - 0.5 * root[...].astype(F32)).astype(BF16)
        inv[...] = fac[...]
        root[...] = dot(root[...], fac[...]).astype(BF16)
        for _ in range(2):
            fac[...] = (1.5 * eye(MEMBERS) - 0.5 * dot(inv[...], root[...])).astype(BF16)
            root[...] = dot(root[...], fac[...]).astype(BF16)
            inv[...] = dot(fac[...], inv[...]).astype(BF16)
        fac[...] = (1.5 * eye(MEMBERS) - 0.5 * dot(inv[...], root[...])).astype(BF16)
        upper = dot(fac[:HALF], inv[...]).astype(BF16)
        corner = dot(fac[HALF:], inv[:, HALF:]).astype(BF16)
        blocks = (upper[:, :HALF], upper[:, HALF:], corner)
        right = rhs_part[r, 0] + rhs_in[r, 1] + rhs_in[r, 2] + rhs_in[r, 3]
        right = jnp.concatenate([right, right], axis=0)
        half_way = sym_rows(right, blocks)
        mwbuf[r, 0] = (sym_rows(half_way, blocks) * per)[0:8]
        gain = jnp.sqrt((MEMBERS - 1.0) * per)
        for b in range(3):
            scaled = (blocks[b].astype(F32) * gain).astype(BF16)
            for h in range(2):
                vbuf[r, 0, h, b] = scaled[h * 128 : (h + 1) * 128]
        gathers[r, 3] = zcopy(vbuf.at[r, 0], vbuf.at[r, 3], 1, r, 9)
        gathers[r, 1] = zcopy(vbuf.at[r, 0], vbuf.at[r, 1], 3, r, 10)
        for q in (1, 2, 3):
            gathers[r, 3 + q] = zcopy(mwbuf.at[r, 0], mwbuf.at[r, 4 - q], q, r, 10 + q)

    forward = {}
    for r in range(ROUNDS):
        gathers[r, 3].wait_recv()
        forward[r, 0] = zcopy(vbuf.at[r, 3, 0], vbuf.at[r, 2, 0], 1, r, 14)
        gathers[r, 1].wait_recv()
        forward[r, 1] = zcopy(vbuf.at[r, 1, 1], vbuf.at[r, 2, 1], 3, r, 15)

    def gcopy(phase, s, source_ref, target_ref):
        return pltpu.make_async_remote_copy(
            src_ref=source_ref,
            dst_ref=target_ref,
            send_sem=send_g.at[phase, s],
            recv_sem=recv_g.at[phase, s],
            device_id={"grp": peer(s)},
            device_id_type=MESH,
        )

    locals_ = []
    routed = []
    for r in range(ROUNDS):
        for q in (0, 1, 3, 2):
            if q == 1:
                for p in (1, 2, 3):
                    gathers[r, 3 + p].wait_recv()
            if q == 2:
                forward[r, 0].wait_recv()
                forward[r, 1].wait_recv()
            g = group(r, q)
            left, right = pert[g, :, :HALF], pert[g, :, HALF:]
            v = [vbuf[r, q, :, b].reshape(HALF, HALF) for b in range(3)]
            shift = jnp.sum(pert[g].astype(F32) * mwbuf[r, q][0:1], axis=1, keepdims=True)
            shift = shift + mean[g][:, 0:1]
            cols = (
                dot(left, v[0]) + dot_nt(right, v[1]) + shift,
                dot(left, v[1]) + dot(right, v[2]) + shift,
            )
            for h in range(2):
                block = cols[h].astype(BF16)
                for b in range(16):
                    spread[r, h * 16 + b, zpeer(q)] = block[b * 16 : (b + 1) * 16]
        for s in ORDER:
            copy = gcopy(r, s, spread.at[r, peer(s)], gathered.at[pl.ds(r * 128 + me * 4, 4)])
            copy.start()
            routed.append(copy)
        mine = pltpu.make_async_copy(
            spread.at[r, me], gathered.at[pl.ds(r * 128 + me * 4, 4)], self_sem.at[r]
        )
        mine.start()
        locals_.append(mine)
    for copy in routed:
        copy.wait_recv()
    for copy in locals_:
        copy.wait()

    row = pl.multiple_of(lax.rem(me, 16) * 16, 16)
    col = pl.multiple_of((me // 16) * HALF, HALF)
    final = []

    def pick(s):
        d = peer(s)
        for k in range(GROUPS_HERE):
            picked[d, k] = gathered[holder[d * GROUPS_HERE + k]]

    def send(s):
        target = out.at[:, pl.ds(row, 16), pl.ds(col, HALF)]
        if s == 0:
            copy = pltpu.make_async_copy(picked.at[me], target, self_sem.at[2])
        else:
            copy = gcopy(2, s, picked.at[peer(s)], target)
        copy.start()
        final.append(copy)

    order = ORDER + [0]
    pick(order[0])
    for n in range(GRP):
        if n + 1 < GRP:
            pick(order[n + 1])
        send(order[n])
    for copy in pending + routed:
        copy.wait_send()
    for copy in final:
        copy.wait()


def analyse(background, obs_ens, innovation, obs_weight, obs_count, holder):
    vmem = pltpu.VMEM
    any_spec = pl.BlockSpec(memory_space=pl.ANY)
    vmem_spec = pl.BlockSpec(memory_space=pltpu.VMEM)
    return pl.pallas_call(
        kernel,
        out_shape=jax.ShapeDtypeStruct(background.shape, BF16),
        in_specs=[
            pl.BlockSpec(memory_space=pltpu.SMEM), any_spec, any_spec,
            vmem_spec, vmem_spec, vmem_spec,
        ],
        out_specs=any_spec,
        scratch_shapes=[
            vmem((8, 512, 512), BF16),
            vmem((8, 256, 512), BF16),
            vmem((8, 8, 512), F32),
            vmem((8, 16, 512), BF16),
            vmem((2, 4, 2, 3, 128, 256), BF16),
            vmem((2, 3, 256, 256), F32),
            vmem((2, 2, 3, 128, 256), F32),
            vmem((2, 2, 3, 128, 256), BF16),
            vmem((2, 2, 2, 3, 128, 256), BF16),
            vmem((2, 4, 8, 512), F32),
            vmem((2, 4, 8, 512), F32),
            vmem((512, 512), BF16),
            vmem((512, 512), BF16),
            vmem((512, 512), BF16),
            vmem((2, 4, 2, 3, 128, 256), BF16),
            vmem((2, 4, 8, 512), F32),
            vmem((8, 256, 512), BF16),
            vmem((8, 256, 128), F32),
            vmem((2, 32, 4, 16, 256), BF16),
            vmem((256, 16, 256), BF16),
            vmem((32, 8, 16, 256), BF16),
            pltpu.SemaphoreType.DMA((2, 4)),
            pltpu.SemaphoreType.DMA,
            pltpu.SemaphoreType.DMA((2, 16)),
            pltpu.SemaphoreType.DMA((2, 16)),
            pltpu.SemaphoreType.DMA((3, 32)),
            pltpu.SemaphoreType.DMA((3, 32)),
            pltpu.SemaphoreType.DMA((3,)),
        ],
        compiler_params=pltpu.CompilerParams(
            collective_id=0, has_side_effects=True, vmem_limit_bytes=60 * 1024 * 1024
        ),
    )(holder, obs_ens, background, innovation, obs_weight, obs_count)


def holder_index(dest, local_groups):
    group_total = dest.shape[0]
    group_ids = jnp.arange(group_total, dtype=jnp.int32)
    same_dest = dest[None, :] == dest[:, None]
    earlier = group_ids[None, :] < group_ids[:, None]
    arrival_rank = jnp.sum(jnp.where(same_dest & earlier, 1, 0), axis=1).astype(jnp.int32)
    slot_of = dest * local_groups + arrival_rank
    local = group_ids % local_groups
    place = (local % ROUNDS) * 128 + (group_ids // local_groups) * 4 + local // ROUNDS
    return jnp.sum(
        jnp.where(slot_of[None, :] == group_ids[:, None], place[None, :], 0), axis=1
    ).astype(jnp.int32)


def body(background, obs_ens, innovation, obs_weight, obs_count, dest):
    holder = holder_index(dest, background.shape[0])
    return analyse(background, obs_ens, innovation, obs_weight, obs_count, holder)


def solution(mesh):
    return jax.shard_map(
        body,
        mesh=mesh,
        in_specs=(
            P("grp", "own", None),
            P("grp", "own", None),
            P("grp", "own"),
            P("grp", "own"),
            P("grp", "own"),
            P(),
        ),
        out_specs=P("grp", "own", None),
        check_vma=False,
    )
```

time: 255 us -> 121 us (0.47)
  waiting for transfers between devices: 138 us -> 0 us
  Pallas kernels: 0 us -> 114 us
  blocking collectives: 49.3 us -> 0 us
  matrix products: 26.3 us -> 0 us
  between operations: 14.3 us -> 0.02 us
  starting transfers between devices: 7.87 us -> 0 us
  other arithmetic: 8.6 us -> 2.34 us
  local copies, waits for them, and re-layouts: 9.52 us -> 4.37 us
    pallas_call x0 -> x1, Pallas kernels: none -> 114 us  [analyse(): pl.pallas_call(kernel, out_shape=jax.ShapeDtypeStruct(background.shape, B...]
    reduce_scatter x1 -> x0, waiting for transfers between devices: 62.8 us -> none  [solve_weights(): lax.psum_scatter(gram_local, 'own', scatter_dimension=0, tiled=True)]
    all_gather x1 -> x0, waiting for transfers between devices: 47.5 us -> none  [solve_weights(): lax.all_gather(newton_weights(gram_part, right_part), 'own', axis=0, tile...]
    all_to_all x1 -> x0, blocking collectives: 32.8 us -> none  [route(): lax.all_to_all(ordered, 'grp', split_axis=0, concat_axis=0, tiled=True)]
    all_to_all x1 -> x0, waiting for transfers between devices: 28.1 us -> none  [route(): lax.all_to_all(pieces, 'grp', split_axis=0, concat_axis=0, tiled=True)]
    dot_general x15 -> x0, matrix products: 26.3 us -> none  [the longest x1 6.28 us: solve_weights(): jnp.einsum('gpk,gpl->gkl', weighted, obs_pert, preferred_element_type=jnp...]
    unnamed x1 -> x0, blocking collectives: 16.5 us -> none
    all_to_all x1 -> x0, starting transfers between devices: 7.83 us -> none  [route(): lax.all_to_all(pieces, 'grp', split_axis=0, concat_axis=0, tiled=True)]
  transfers between devices with their start and end apart: 3 -> 0, of which waited for: 3 -> 0; matrix products, arithmetic and copies ran while one was open for 2% -> 0% of each run, Pallas kernels for 0% -> 0%
where the time goes in v2:
time: 121 us
  Pallas kernels  114 us (94%)
  local copies, waits for them, and re-layouts  4.37 us (4%)
  other arithmetic  2.34 us (2%)
    pallas_call x1, Pallas kernels, analyse(): pl.pallas_call(kernel, out_shape=jax.ShapeDtypeStruct(background.shape, B...  114 us
    unnamed x2, local copies, waits for them, and re-layouts  4.37 us

profile of v2, /device:TPU:1, one launch (start us, length us, event | category | flops | bytes accessed | tf_op | source)
XLA Modules:
  0.0 120.8 jit_solution(11788822571360157146)
XLA Ops:
  0.0 0.9 select_reduce_fusion.1
  0.9 0.7 fusion.5
  1.6 0.7 select_reduce_fusion.holder
  2.3 1.3 %copy.8.count = s32[8,1]{1,0:T(8,128)} copy(s32[8,1]{0,1:T(1,128)} %param.10) | data formatting | bytes 64 | tf_op args[4]
  3.7 114.0 %shard_map.64 = bf16[8,256,512]{2,1,0:T(8,128)(2,1)} custom-call(s32[256]{0:T(256)} %select_reduce_fusion.holder, bf16[8,512,512]{2,1,0:T(8,128)(2,1)} %obs_hbm.1, bf16[8,256,512]{2,1,0:T(8,128)(2,1)} %bg_hbm.1, bf16[8,512]{1,0:T(8,128)(2,1)} %innov.1, bf16[8,512]{1,0:T(8,128)(2,1)} %obs_weight.1, s32[8,1]{1,0:T(8,128)} %copy.8.count), custom_call_target="tpu_custom_call" | custom-call | tf_op jit(solution)/shard_map/pallas_call | solution.py:306
  117.7 3.0 %copy.10 = bf16[8,256,512]{2,1,0:T(8,128)(2,1)} copy(bf16[8,256,512]{2,1,0:T(8,128)(2,1)} %shard_map.64) | data formatting | bytes 4194304

commit v3 on v2

v3 whole, which is shorter than its diff:
```python
import jax
import jax.numpy as jnp
from jax import lax
from jax.experimental import pallas as pl
from jax.experimental.pallas import tpu as pltpu
from jax.sharding import PartitionSpec as P

MESH = pl.DeviceIdType.MESH
F32 = jnp.float32
BF16 = jnp.bfloat16
MEMBERS = 512
B = 128
GROUPS_HERE = 8
ROUNDS = 2
GRP = 32
STRIDE = 12
BLOCKS = [(i, j) for i in range(4) for j in range(i, 4)]


def dot(a, b):
    return jnp.dot(a, b, preferred_element_type=F32)


def dot_nt(a, b):
    return lax.dot_general(a, b, (((1,), (1,)), ((), ())), preferred_element_type=F32)


def eye(n):
    rows = lax.broadcasted_iota(jnp.int32, (n, n), 0)
    cols = lax.broadcasted_iota(jnp.int32, (n, n), 1)
    return jnp.where(rows == cols, 1.0, 0.0).astype(F32)


def span(i):
    return slice(i * B, (i + 1) * B)


def kernel(
    dest_hbm, obs_hbm, bg_hbm, innov_hbm, weight_hbm, count_hbm, out,
    dest, innov, obs_weight, count,
    obs, bg, wrow, src, part, own_part, relay_own, relay_in, owner_in, rhs_part, rhs_in,
    root, inv, fac, full, vbuf, mwbuf, pert, mean, spread, gathered, picked, holder_v, holder,
    obs_sem, bg_sem, send_z, recv_z, send_g, recv_g, self_sem, small_sem,
):
    me = lax.axis_index("grp")
    z = lax.axis_index("own")
    y, x, c = me // 8, lax.rem(me // 2, 4), lax.rem(me, 2)

    def peer(s):
        return (
            lax.rem(y + s // 8, 4) * 8
            + lax.rem(x + lax.rem(s // 2, 4), 4) * 2
            + lax.rem(c + lax.rem(s, 2), 2)
        )

    def step(i):
        return 1 + lax.rem(i * STRIDE, GRP - 1)

    def zpeer(q):
        return lax.rem(z + q, 4)

    def group(r, q):
        return zpeer(q) * ROUNDS + r

    barrier = pltpu.get_barrier_semaphore()

    def greet(s, carry):
        pl.semaphore_signal(barrier, inc=1, device_id={"grp": peer(s)}, device_id_type=MESH)
        return carry

    for q in (2, 1, 3):
        pl.semaphore_signal(barrier, inc=1, device_id={"own": zpeer(q)}, device_id_type=MESH)
    lax.fori_loop(1, GRP, greet, 0)

    small = (
        (count_hbm, count), (weight_hbm, obs_weight), (innov_hbm, innov), (dest_hbm, dest)
    )
    small = [
        pltpu.make_async_copy(pair[0], pair[1], small_sem.at[n]) for n, pair in enumerate(small)
    ]
    for load in small:
        load.start()
    loads = {}
    for r in range(ROUNDS):
        for q in (2, 1, 3, 0):
            loads[r, q] = pltpu.make_async_copy(
                obs_hbm.at[group(r, q)], obs.at[group(r, q)], obs_sem.at[r, q]
            )
            loads[r, q].start()
    bg_load = pltpu.make_async_copy(bg_hbm, bg, bg_sem)
    bg_load.start()

    for load in small:
        load.wait()
    position = lax.broadcasted_iota(jnp.int32, (1, 512), 1)
    for g in range(GROUPS_HERE):
        live = position < count[:, g : g + 1]
        weight = jnp.where(live, obs_weight[g : g + 1].astype(F32), 0.0)
        source = (weight * innov[g : g + 1].astype(F32)).astype(BF16).astype(F32)
        wrow[g] = jnp.broadcast_to(weight, (8, 512))
        src[g] = jnp.broadcast_to(source, (16, 512)).astype(BF16)

    pending = []

    def zcopy(source_ref, target_ref, q, r, index):
        copy = pltpu.make_async_remote_copy(
            src_ref=source_ref,
            dst_ref=target_ref,
            send_sem=send_z.at[r, index],
            recv_sem=recv_z.at[r, index],
            device_id={"own": zpeer(q)},
            device_id_type=MESH,
        )
        copy.start()
        pending.append(copy)
        return copy

    def gram(r, q):
        loads[r, q].wait()
        g = group(r, q)
        ens = obs[g].astype(F32)
        centred = (ens - jnp.mean(ens, axis=1, keepdims=True)).astype(BF16)
        turned = (centred.astype(F32).T * wrow[g][0:1]).astype(BF16)
        rhs_part[r, q] = dot(src[g], centred)[0:8]
        for i in range(4):
            strip = dot(turned[span(i)], centred[:, i * B :])
            for j in range(i, 4):
                b = BLOCKS.index((i, j))
                h, k = b // 5, b % 5
                block = strip[:, (j - i) * B : (j - i + 1) * B]
                if q == 0:
                    own_part[r, b] = block
                elif (q, h) in ((1, 0), (3, 1)):
                    relay_own[r, h, k] = block
                else:
                    part[r, q, h, k] = block.astype(BF16)

    relay = {}
    direct = {}

    def send_parts(r, q):
        if q == 2:
            relay[r, 0] = zcopy(part.at[r, 2, 0], relay_in.at[r, 0], 1, r, 0)
            relay[r, 1] = zcopy(part.at[r, 2, 1], relay_in.at[r, 1], 3, r, 1)
        elif q == 1:
            direct[r, 1] = zcopy(part.at[r, 1, 1], owner_in.at[r, 0, 1], 1, r, 2)
        else:
            direct[r, 0] = zcopy(part.at[r, 3, 0], owner_in.at[r, 1, 0], 3, r, 3)
        direct[r, 1 + q] = zcopy(rhs_part.at[r, q], rhs_in.at[r, q], q, r, 3 + q)

    combined = {}

    def combine(r):
        for h, q in ((0, 1), (1, 3)):
            relay[r, h].wait_recv()
            part[r, q, h] = (relay_own[r, h] + relay_in[r, h].astype(F32)).astype(BF16)
            combined[r, h] = zcopy(
                part.at[r, q, h], owner_in.at[r, 0 if q == 1 else 1, h], q, r, 7 + h
            )

    gathers = {}
    forward = {}

    def newton(r):
        for h in range(2):
            direct[r, h].wait_recv()
            combined[r, h].wait_recv()
        for q in (1, 2, 3):
            direct[r, 1 + q].wait_recv()
        squares = jnp.zeros((B, B), F32)
        totals = []
        for b, (i, j) in enumerate(BLOCKS):
            h, k = b // 5, b % 5
            total = own_part[r, b] + owner_in[r, 0, h, k].astype(F32)
            total = total + owner_in[r, 1, h, k].astype(F32)
            if i == j:
                total = total + (MEMBERS - 1.0) * eye(B)
                squares = squares + total * total
            else:
                squares = squares + 2.0 * (total * total)
            own_part[r, b] = total
        scale = jnp.sqrt(jnp.full((1, 1), jnp.sum(squares), F32))
        per = 1.0 / scale
        for b, (i, j) in enumerate(BLOCKS):
            block = own_part[r, b] * per
            root[span(i), span(j)] = block.astype(BF16)
            if i != j:
                root[span(j), span(i)] = block.T.astype(BF16)
        fac[...] = (1.5 * eye(MEMBERS) - 0.5 * root[...].astype(F32)).astype(BF16)
        inv[...] = fac[...]
        root[...] = dot(root[...], fac[...]).astype(BF16)
        for _ in range(2):
            fac[...] = (1.5 * eye(MEMBERS) - 0.5 * dot(inv[...], root[...])).astype(BF16)
            root[...] = dot(root[...], fac[...]).astype(BF16)
            inv[...] = dot(fac[...], inv[...]).astype(BF16)
        fac[...] = (1.5 * eye(MEMBERS) - 0.5 * dot(inv[...], root[...])).astype(BF16)
        inv[...] = dot(fac[...], inv[...]).astype(BF16)

        def through(rows):
            high = rows.astype(BF16)
            low = (rows - high.astype(F32)).astype(BF16)
            both = dot_nt(jnp.concatenate([high, low], axis=0), inv[...])
            return both[0:16] + both[16:32]

        right = rhs_part[r, 0] + rhs_in[r, 1] + rhs_in[r, 2] + rhs_in[r, 3]
        right = jnp.concatenate([right, right], axis=0)
        mwbuf[r, 0] = (through(through(right)) * per)[0:8]
        gain = jnp.sqrt((MEMBERS - 1.0) * per)
        for b, (i, j) in enumerate(BLOCKS):
            vbuf[r, 0, b // 5, b % 5] = (inv[span(i), span(j)].astype(F32) * gain).astype(BF16)

    def gather(r):
        gathers[r, 3] = zcopy(vbuf.at[r, 0], vbuf.at[r, 3], 1, r, 9)
        gathers[r, 1] = zcopy(vbuf.at[r, 0], vbuf.at[r, 1], 3, r, 10)
        for q in (1, 2, 3):
            gathers[r, 3 + q] = zcopy(mwbuf.at[r, 0], mwbuf.at[r, 4 - q], q, r, 10 + q)

    def pass_on(r):
        gathers[r, 3].wait_recv()
        forward[r, 0] = zcopy(vbuf.at[r, 3, 0], vbuf.at[r, 2, 0], 1, r, 14)
        gathers[r, 1].wait_recv()
        forward[r, 1] = zcopy(vbuf.at[r, 1, 1], vbuf.at[r, 2, 1], 3, r, 15)
        for q in (1, 2, 3):
            gathers[r, 3 + q].wait_recv()

    def perturb():
        bg_load.wait()

        def one(g, carry):
            state = bg[g].astype(F32)
            centre = jnp.mean(state, axis=1, keepdims=True)
            pert[g] = (state - centre).astype(BF16)
            mean[g] = jnp.broadcast_to(centre, (256, B))
            return carry

        lax.fori_loop(0, GROUPS_HERE, one, 0)

    def index():
        total = GROUPS_HERE * GRP
        across = jnp.broadcast_to(dest[...], (total, total))
        down = across.T
        rows = lax.broadcasted_iota(jnp.int32, (total, total), 0)
        cols = lax.broadcasted_iota(jnp.int32, (total, total), 1)
        match = jnp.where((across == down) & (cols < rows), 1, 0)
        slot = down * GROUPS_HERE + jnp.sum(match, axis=1, keepdims=True)
        local = lax.rem(rows, GROUPS_HERE)
        owner = lax.rem(local // ROUNDS + 4 - z, 4)
        place = (lax.rem(local, ROUNDS) * 4 + owner) * GRP + rows // GROUPS_HERE
        chosen = jnp.where(slot == cols, place, 0)
        holder_v[...] = jnp.broadcast_to(jnp.sum(chosen, axis=0, keepdims=True), (8, total))
        copy = pltpu.make_async_copy(holder_v, holder, small_sem.at[4])
        copy.start()
        copy.wait()

    def gcopy(phase, s, source_ref, target_ref):
        return pltpu.make_async_remote_copy(
            src_ref=source_ref,
            dst_ref=target_ref,
            send_sem=send_g.at[phase, s],
            recv_sem=recv_g.at[phase, s],
            device_id={"grp": peer(s)},
            device_id_type=MESH,
        )

    def spread_copy(e, s):
        return gcopy(e, s, spread.at[e, peer(s)], gathered.at[e * GRP + me])

    def apply(r, q):
        g = group(r, q)
        e = r * 4 + q
        for b, (i, j) in enumerate(BLOCKS):
            block = vbuf[r, q, b // 5, b % 5]
            full[span(i), span(j)] = block
            if i != j:
                full[span(j), span(i)] = block.T
        shift = jnp.sum(pert[g].astype(F32) * mwbuf[r, q][0:1], axis=1, keepdims=True)
        shift = shift + mean[g][:, 0:1]
        for h in range(2):
            block = (dot(pert[g], full[:, h * 256 : (h + 1) * 256]) + shift).astype(BF16)
            for k in range(16):
                spread[e, h * 16 + k] = block[k * 16 : (k + 1) * 16]

        def launch(i, carry):
            spread_copy(e, step(i)).start()
            return carry

        lax.fori_loop(0, GRP - 1, launch, 0)
        mine = pltpu.make_async_copy(
            spread.at[e, me], gathered.at[e * GRP + me], self_sem.at[e]
        )
        mine.start()
        locals_.append(mine)

    locals_ = []
    for q in (2, 1, 3):
        gram(0, q)
        if q == 2:
            pl.semaphore_wait(barrier, GRP - 1 + 3)
        send_parts(0, q)
    gram(0, 0)
    for q in (2, 1, 3, 0):
        gram(1, q)
    combine(0)
    for q in (2, 1, 3):
        send_parts(1, q)
    perturb()
    index()
    newton(0)
    combine(1)
    gather(0)
    apply(0, 0)
    newton(1)
    gather(1)
    apply(1, 0)
    pass_on(0)
    apply(0, 1)
    apply(0, 3)
    pass_on(1)
    apply(1, 1)
    apply(1, 3)
    for r in range(ROUNDS):
        forward[r, 0].wait_recv()
        forward[r, 1].wait_recv()
        apply(r, 2)

    def landed(e, carry):
        def one(s, inner):
            spread_copy(e, s).wait_recv()
            return inner

        return lax.fori_loop(1, GRP, one, carry)

    lax.fori_loop(0, GROUPS_HERE, landed, 0)
    for copy in locals_:
        copy.wait()

    row = pl.multiple_of(lax.rem(me, 16) * 16, 16)
    col = pl.multiple_of((me // 16) * 256, 256)
    target = out.at[:, pl.ds(row, 16), pl.ds(col, 256)]

    def pick(d):
        for k in range(GROUPS_HERE):
            at = lax.clamp(0, holder[0, d * GROUPS_HERE + k], GROUPS_HERE * GRP - 1)
            picked[d, k] = gathered[at]

    def route(s):
        return gcopy(GROUPS_HERE, s, picked.at[peer(s)], target)

    pick(peer(step(0)))

    def move(i, carry):
        pick(peer(step(i + 1)))
        route(step(i)).start()
        return carry

    lax.fori_loop(0, GRP - 2, move, 0)
    pick(me)
    route(step(GRP - 2)).start()
    last = pltpu.make_async_copy(picked.at[me], target, self_sem.at[GROUPS_HERE])
    last.start()
    for copy in pending:
        copy.wait_send()

    def sent(e, carry):
        def one(s, inner):
            spread_copy(e, s).wait_send()
            return inner

        return lax.fori_loop(1, GRP, one, carry)

    lax.fori_loop(0, GROUPS_HERE, sent, 0)

    def done(s, carry):
        route(s).wait()
        return carry

    lax.fori_loop(1, GRP, done, 0)
    last.wait()


def analyse(background, obs_ens, innovation, obs_weight, obs_count, dest):
    vmem = pltpu.VMEM
    hbm_spec = pl.BlockSpec(memory_space=pltpu.HBM)
    return pl.pallas_call(
        kernel,
        out_shape=jax.ShapeDtypeStruct(background.shape, BF16),
        in_specs=[hbm_spec] * 6,
        out_specs=pl.BlockSpec(memory_space=pl.ANY),
        scratch_shapes=[
            vmem(dest.shape, jnp.int32),
            vmem(innovation.shape, BF16),
            vmem(obs_weight.shape, BF16),
            vmem(obs_count.shape, jnp.int32),
            vmem((8, 512, 512), BF16),
            vmem((8, 256, 512), BF16),
            vmem((8, 8, 512), F32),
            vmem((8, 16, 512), BF16),
            vmem((2, 4, 2, 5, B, B), BF16),
            vmem((2, 10, B, B), F32),
            vmem((2, 2, 5, B, B), F32),
            vmem((2, 2, 5, B, B), BF16),
            vmem((2, 2, 2, 5, B, B), BF16),
            vmem((2, 4, 8, 512), F32),
            vmem((2, 4, 8, 512), F32),
            vmem((512, 512), BF16),
            vmem((512, 512), BF16),
            vmem((512, 512), BF16),
            vmem((512, 512), BF16),
            vmem((2, 4, 2, 5, B, B), BF16),
            vmem((2, 4, 8, 512), F32),
            vmem((8, 256, 512), BF16),
            vmem((8, 256, B), F32),
            vmem((8, 32, 16, 256), BF16),
            vmem((256, 16, 256), BF16),
            vmem((32, 8, 16, 256), BF16),
            vmem((8, 256), jnp.int32),
            pltpu.SMEM((8, 256), jnp.int32),
            pltpu.SemaphoreType.DMA((2, 4)),
            pltpu.SemaphoreType.DMA,
            pltpu.SemaphoreType.DMA((2, 16)),
            pltpu.SemaphoreType.DMA((2, 16)),
            pltpu.SemaphoreType.DMA((9, 32)),
            pltpu.SemaphoreType.DMA((9, 32)),
            pltpu.SemaphoreType.DMA((9,)),
            pltpu.SemaphoreType.DMA((5,)),
        ],
        compiler_params=pltpu.CompilerParams(
            collective_id=0, has_side_effects=True, vmem_limit_bytes=44 * 1024 * 1024
        ),
    )(*(
        pltpu.with_memory_space_constraint(a, pltpu.HBM)
        for a in (dest, obs_ens, background, innovation, obs_weight, obs_count)
    ))


def body(background, obs_ens, innovation, obs_weight, obs_count, dest):
    return analyse(
        background, obs_ens, innovation, obs_weight, obs_count.T, dest.reshape(1, -1)
    )


def solution(mesh):
    return jax.shard_map(
        body,
        mesh=mesh,
        in_specs=(
            P("grp", "own", None),
            P("grp", "own", None),
            P("grp", "own"),
            P("grp", "own"),
            P("grp", "own"),
            P(),
        ),
        out_specs=P("grp", "own", None),
        check_vma=False,
    )
```

time: 121 us -> 97.5 us (0.81)
  Pallas kernels: 114 us -> 95.7 us
  local copies, waits for them, and re-layouts: 4.37 us -> 1.32 us
  other arithmetic: 2.34 us -> 0 us
    pallas_call x1, Pallas kernels: 114 us -> 95.7 us  [analyse(): pl.pallas_call(kernel, out_shape=jax.ShapeDtypeStruct(background.shape, B...]
    unnamed x2 -> x1, local copies, waits for them, and re-layouts: 4.37 us -> 1.32 us
    reduce_sum x2 -> x0, other arithmetic: 1.65 us -> none  [the longest x1 0.93 us: holder_index(): jnp.sum(jnp.where(same_dest & earlier, 1, 0), axis=1).astype(jnp.int32)]
where the time goes in v3:
time: 97.5 us; the launch traced here: 97 us
  Pallas kernels  95.7 us (98%)
  local copies, waits for them, and re-layouts  1.32 us (1%)
    pallas_call x1, Pallas kernels, analyse(): pl.pallas_call(kernel, out_shape=jax.ShapeDtypeStruct(background.shape, B...  95.7 us

profile of v3, /device:TPU:1, one launch (start us, length us, event | category | flops | bytes accessed | tf_op | source)
XLA Modules:
  0.0 97.0 jit_solution(17820474422497806926)
XLA Ops:
  0.0 95.7 %shard_map.64 = bf16[8,256,512]{2,1,0:T(8,128)(2,1)S(1)} custom-call(s32[1,256]{1,0:T(1,128)} %bitcast.2, bf16[8,512,512]{2,1,0:T(8,128)(2,1)} %obs_hbm.1, bf16[8,256,512]{2,1,0:T(8,128)(2,1)} %bg_hbm.1, bf16[8,512]{1,0:T(8,128)(2,1)} %innov_hbm.1, bf16[8,512]{1,0:T(8,128)(2,1)} %weight_hbm.1, s32[1,8]{1,0:T(1,128)} %bitcast.3), custom_call_target="tpu_custom_call" | custom-call | tf_op jit(solution)/shard_map/pallas_call | solution.py:384
  95.7 1.3 %copy.8 = bf16[8,256,512]{2,1,0:T(8,128)(2,1)} copy(bf16[8,256,512]{2,1,0:T(8,128)(2,1)S(1)} %shard_map.64) | data formatting | bytes 4194304

commit v4 on v3

--- a/solution.py
+++ b/solution.py
@@ -14,7 +14,8 @@
 ROUNDS = 2
 GRP = 32
 STRIDE = 12
-BLOCKS = [(i, j) for i in range(4) for j in range(i, 4)]
+OFF = [(0, 1), (0, 2), (0, 3), (1, 2), (1, 3), (2, 3)]
+HALF = 4
 
 
 def dot(a, b):
@@ -29,6 +30,39 @@
     rows = lax.broadcasted_iota(jnp.int32, (n, n), 0)
     cols = lax.broadcasted_iota(jnp.int32, (n, n), 1)
     return jnp.where(rows == cols, 1.0, 0.0).astype(F32)
+
+
+def masks():
+    rows = lax.broadcasted_iota(jnp.int32, (B, B), 0)
+    cols = lax.broadcasted_iota(jnp.int32, (B, B), 1)
+    return rows <= cols, rows == cols
+
+
+def pack_diagonals(d):
+    upper, middle = masks()
+    pairs = [jnp.where(upper, d[i], d[i + 1]) for i in (0, 2)]
+    lines = [jnp.sum(jnp.where(middle, d[i], 0.0), axis=0, keepdims=True) for i in (1, 3)]
+    return pairs, lines
+
+
+def unpack_diagonals(pairs, lines):
+    upper, middle = masks()
+    out = []
+    for pair, line in zip(pairs, lines):
+        turned = pair.T
+        out.append(jnp.where(upper, pair, turned))
+        out.append(jnp.where(middle, line, jnp.where(upper, turned, pair)))
+    return out
+
+
+def tile(row, lines):
+    parts = [row[:, span(i)] for i in range(4)] + lines + [jnp.zeros((2, B), F32)]
+    return jnp.concatenate(parts, axis=0)
+
+
+def untile(small):
+    row = jnp.concatenate([small[i : i + 1] for i in range(4)], axis=1)
+    return row, [small[4:5], small[5:6]]
 
 
 def span(i):
@@ -121,19 +155,23 @@
         ens = obs[g].astype(F32)
         centred = (ens - jnp.mean(ens, axis=1, keepdims=True)).astype(BF16)
         turned = (centred.astype(F32).T * wrow[g][0:1]).astype(BF16)
-        rhs_part[r, q] = dot(src[g], centred)[0:8]
+        diagonal = []
+        blocks = {}
         for i in range(4):
             strip = dot(turned[span(i)], centred[:, i * B :])
-            for j in range(i, 4):
-                b = BLOCKS.index((i, j))
-                h, k = b // 5, b % 5
-                block = strip[:, (j - i) * B : (j - i + 1) * B]
-                if q == 0:
-                    own_part[r, b] = block
-                elif (q, h) in ((1, 0), (3, 1)):
-                    relay_own[r, h, k] = block
-                else:
-                    part[r, q, h, k] = block.astype(BF16)
+            diagonal.append(strip[:, :B])
+            for j in range(i + 1, 4):
+                blocks[i, j] = strip[:, (j - i) * B : (j - i + 1) * B]
+        pairs, lines = pack_diagonals(diagonal)
+        rhs_part[r, q] = tile(dot(src[g], centred)[0:1], lines)
+        for b, block in enumerate([blocks[ij] for ij in OFF] + pairs):
+            h, k = b // HALF, b % HALF
+            if q == 0:
+                own_part[r, b] = block
+            elif (q, h) in ((1, 0), (3, 1)):
+                relay_own[r, h, k] = block
+            else:
+                part[r, q, h, k] = block.astype(BF16)
 
     relay = {}
     direct = {}
@@ -167,25 +205,28 @@
             combined[r, h].wait_recv()
         for q in (1, 2, 3):
             direct[r, 1 + q].wait_recv()
+        small = rhs_part[r, 0] + rhs_in[r, 1] + rhs_in[r, 2] + rhs_in[r, 3]
+        right, lines = untile(small)
         squares = jnp.zeros((B, B), F32)
-        totals = []
-        for b, (i, j) in enumerate(BLOCKS):
-            h, k = b // 5, b % 5
+        for b in range(2 * HALF):
+            h, k = b // HALF, b % HALF
             total = own_part[r, b] + owner_in[r, 0, h, k].astype(F32)
             total = total + owner_in[r, 1, h, k].astype(F32)
-            if i == j:
-                total = total + (MEMBERS - 1.0) * eye(B)
-                squares = squares + total * total
-            else:
+            own_part[r, b] = total
+            if b < len(OFF):
                 squares = squares + 2.0 * (total * total)
-            own_part[r, b] = total
+        diagonal = unpack_diagonals([own_part[r, 6], own_part[r, 7]], lines)
+        diagonal = [d + (MEMBERS - 1.0) * eye(B) for d in diagonal]
+        for d in diagonal:
+            squares = squares + d * d
         scale = jnp.sqrt(jnp.full((1, 1), jnp.sum(squares), F32))
         per = 1.0 / scale
-        for b, (i, j) in enumerate(BLOCKS):
+        for i in range(4):
+            root[span(i), span(i)] = (diagonal[i] * per).astype(BF16)
+        for b, (i, j) in enumerate(OFF):
             block = own_part[r, b] * per
             root[span(i), span(j)] = block.astype(BF16)
-            if i != j:
-                root[span(j), span(i)] = block.T.astype(BF16)
+            root[span(j), span(i)] = block.T.astype(BF16)
         fac[...] = (1.5 * eye(MEMBERS) - 0.5 * root[...].astype(F32)).astype(BF16)
         inv[...] = fac[...]
         root[...] = dot(root[...], fac[...]).astype(BF16)
@@ -202,12 +243,16 @@
             both = dot_nt(jnp.concatenate([high, low], axis=0), inv[...])
             return both[0:16] + both[16:32]
 
-        right = rhs_part[r, 0] + rhs_in[r, 1] + rhs_in[r, 2] + rhs_in[r, 3]
-        right = jnp.concatenate([right, right], axis=0)
-        mwbuf[r, 0] = (through(through(right)) * per)[0:8]
+        weight_row = (through(through(jnp.broadcast_to(right, (16, MEMBERS)))) * per)[0:1]
         gain = jnp.sqrt((MEMBERS - 1.0) * per)
-        for b, (i, j) in enumerate(BLOCKS):
-            vbuf[r, 0, b // 5, b % 5] = (inv[span(i), span(j)].astype(F32) * gain).astype(BF16)
+
+        def scaled(i, j):
+            return inv[span(i), span(j)].astype(F32) * gain
+
+        pairs, lines = pack_diagonals([scaled(i, i) for i in range(4)])
+        mwbuf[r, 0] = tile(weight_row, lines)
+        for b, block in enumerate([scaled(i, j) for i, j in OFF] + pairs):
+            vbuf[r, 0, b // HALF, b % HALF] = block.astype(BF16)
 
     def gather(r):
         gathers[r, 3] = zcopy(vbuf.at[r, 0], vbuf.at[r, 3], 1, r, 9)
@@ -268,12 +313,15 @@
     def apply(r, q):
         g = group(r, q)
         e = r * 4 + q
-        for b, (i, j) in enumerate(BLOCKS):
-            block = vbuf[r, q, b // 5, b % 5]
+        weight_row, lines = untile(mwbuf[r, q])
+        pairs = [vbuf[r, q, 1, 2].astype(F32), vbuf[r, q, 1, 3].astype(F32)]
+        for i, d in enumerate(unpack_diagonals(pairs, lines)):
+            full[span(i), span(i)] = d.astype(BF16)
+        for b, (i, j) in enumerate(OFF):
+            block = vbuf[r, q, b // HALF, b % HALF]
             full[span(i), span(j)] = block
-            if i != j:
-                full[span(j), span(i)] = block.T
-        shift = jnp.sum(pert[g].astype(F32) * mwbuf[r, q][0:1], axis=1, keepdims=True)
+            full[span(j), span(i)] = block.T
+        shift = jnp.sum(pert[g].astype(F32) * weight_row, axis=1, keepdims=True)
         shift = shift + mean[g][:, 0:1]
         for h in range(2):
             block = (dot(pert[g], full[:, h * 256 : (h + 1) * 256]) + shift).astype(BF16)
@@ -395,19 +443,19 @@
             vmem((8, 256, 512), BF16),
             vmem((8, 8, 512), F32),
             vmem((8, 16, 512), BF16),
-            vmem((2, 4, 2, 5, B, B), BF16),
-            vmem((2, 10, B, B), F32),
-            vmem((2, 2, 5, B, B), F32),
-            vmem((2, 2, 5, B, B), BF16),
-            vmem((2, 2, 2, 5, B, B), BF16),
-            vmem((2, 4, 8, 512), F32),
-            vmem((2, 4, 8, 512), F32),
+            vmem((2, 4, 2, HALF, B, B), BF16),
+            vmem((2, 2 * HALF, B, B), F32),
+            vmem((2, 2, HALF, B, B), F32),
+            vmem((2, 2, HALF, B, B), BF16),
+            vmem((2, 2, 2, HALF, B, B), BF16),
+            vmem((2, 4, 8, B), F32),
+            vmem((2, 4, 8, B), F32),
             vmem((512, 512), BF16),
             vmem((512, 512), BF16),
             vmem((512, 512), BF16),
             vmem((512, 512), BF16),
-            vmem((2, 4, 2, 5, B, B), BF16),
-            vmem((2, 4, 8, 512), F32),
+            vmem((2, 4, 2, HALF, B, B), BF16),
+            vmem((2, 4, 8, B), F32),
             vmem((8, 256, 512), BF16),
             vmem((8, 256, B), F32),
             vmem((8, 32, 16, 256), BF16),

time: 97.5 us -> 88.3 us (0.906)
  Pallas kernels: 95.7 us -> 86.6 us
    pallas_call x1, Pallas kernels: 95.7 us -> 86.6 us  [analyse(): pl.pallas_call(kernel, out_shape=jax.ShapeDtypeStruct(background.shape, B...]
where the time goes in v4:
time: 88.3 us; the launch traced here: 88 us
  Pallas kernels  86.6 us (98%)
  local copies, waits for them, and re-layouts  1.32 us (1%)
    pallas_call x1, Pallas kernels, analyse(): pl.pallas_call(kernel, out_shape=jax.ShapeDtypeStruct(background.shape, B...  86.6 us

profile of v4, /device:TPU:1, one launch (start us, length us, event | category | flops | bytes accessed | tf_op | source)
XLA Modules:
  0.0 88.0 jit_solution(4290282979350378919)
XLA Ops:
  0.0 86.6 %shard_map.64 = bf16[8,256,512]{2,1,0:T(8,128)(2,1)S(1)} custom-call(s32[1,256]{1,0:T(1,128)} %bitcast.2, bf16[8,512,512]{2,1,0:T(8,128)(2,1)} %obs_hbm.1, bf16[8,256,512]{2,1,0:T(8,128)(2,1)} %bg_hbm.1, bf16[8,512]{1,0:T(8,128)(2,1)} %innov_hbm.1, bf16[8,512]{1,0:T(8,128)(2,1)} %weight_hbm.1, s32[1,8]{1,0:T(1,128)} %bitcast.3), custom_call_target="tpu_custom_call" | custom-call | tf_op jit(solution)/shard_map/pallas_call | solution.py:432
  86.6 1.3 %copy.8 = bf16[8,256,512]{2,1,0:T(8,128)(2,1)} copy(bf16[8,256,512]{2,1,0:T(8,128)(2,1)S(1)} %shard_map.64) | data formatting | bytes 4194304

commit v5 on v4

--- a/solution.py
+++ b/solution.py
@@ -13,7 +13,8 @@
 GROUPS_HERE = 8
 ROUNDS = 2
 GRP = 32
-STRIDE = 12
+STRIDE = 5
+CORE, SIDE_X, SIDE_Y = (1,), (2, 6), (8, 24)
 OFF = [(0, 1), (0, 2), (0, 3), (1, 2), (1, 3), (2, 3)]
 HALF = 4
 
@@ -74,7 +75,7 @@
     dest, innov, obs_weight, count,
     obs, bg, wrow, src, part, own_part, relay_own, relay_in, owner_in, rhs_part, rhs_in,
     root, inv, fac, full, vbuf, mwbuf, pert, mean, spread, gathered, picked, holder_v, holder,
-    obs_sem, bg_sem, send_z, recv_z, send_g, recv_g, self_sem, small_sem,
+    obs_sem, bg_sem, send_z, recv_z, send_g, recv_g, self_sem, small_sem, known,
 ):
     me = lax.axis_index("grp")
     z = lax.axis_index("own")
@@ -96,33 +97,34 @@
     def group(r, q):
         return zpeer(q) * ROUNDS + r
 
-    barrier = pltpu.get_barrier_semaphore()
-
-    def greet(s, carry):
-        pl.semaphore_signal(barrier, inc=1, device_id={"grp": peer(s)}, device_id_type=MESH)
-        return carry
-
-    for q in (2, 1, 3):
-        pl.semaphore_signal(barrier, inc=1, device_id={"own": zpeer(q)}, device_id_type=MESH)
-    lax.fori_loop(1, GRP, greet, 0)
-
+    loads = {
+        (r, q): pltpu.make_async_copy(
+            obs_hbm.at[group(r, q)], obs.at[group(r, q)], obs_sem.at[r, q]
+        )
+        for r in range(ROUNDS)
+        for q in (2, 1, 3, 0)
+    }
     small = (
         (count_hbm, count), (weight_hbm, obs_weight), (innov_hbm, innov), (dest_hbm, dest)
     )
     small = [
         pltpu.make_async_copy(pair[0], pair[1], small_sem.at[n]) for n, pair in enumerate(small)
     ]
+    bg_load = pltpu.make_async_copy(bg_hbm, bg, bg_sem)
+    barrier = pltpu.get_barrier_semaphore()
+
+    def tell(semaphore, neighbours):
+        for s in neighbours:
+            pl.semaphore_signal(semaphore, inc=1, device_id={"grp": peer(s)}, device_id_type=MESH)
+
+    for q in (2, 1, 3):
+        pl.semaphore_signal(barrier, inc=1, device_id={"own": zpeer(q)}, device_id_type=MESH)
     for load in small:
         load.start()
-    loads = {}
-    for r in range(ROUNDS):
-        for q in (2, 1, 3, 0):
-            loads[r, q] = pltpu.make_async_copy(
-                obs_hbm.at[group(r, q)], obs.at[group(r, q)], obs_sem.at[r, q]
-            )
-            loads[r, q].start()
-    bg_load = pltpu.make_async_copy(bg_hbm, bg, bg_sem)
-    bg_load.start()
+    loads[0, 2].start()
+    tell(barrier, CORE + SIDE_X + SIDE_Y)
+    loads[0, 1].start()
+    loads[0, 3].start()
 
     for load in small:
         load.wait()
@@ -177,6 +179,7 @@
     direct = {}
 
     def send_parts(r, q):
+        direct[r, 1 + q] = zcopy(rhs_part.at[r, q], rhs_in.at[r, q], q, r, 3 + q)
         if q == 2:
             relay[r, 0] = zcopy(part.at[r, 2, 0], relay_in.at[r, 0], 1, r, 0)
             relay[r, 1] = zcopy(part.at[r, 2, 1], relay_in.at[r, 1], 3, r, 1)
@@ -184,7 +187,6 @@
             direct[r, 1] = zcopy(part.at[r, 1, 1], owner_in.at[r, 0, 1], 1, r, 2)
         else:
             direct[r, 0] = zcopy(part.at[r, 3, 0], owner_in.at[r, 1, 0], 3, r, 3)
-        direct[r, 1 + q] = zcopy(rhs_part.at[r, q], rhs_in.at[r, q], q, r, 3 + q)
 
     combined = {}
 
@@ -255,18 +257,18 @@
             vbuf[r, 0, b // HALF, b % HALF] = block.astype(BF16)
 
     def gather(r):
+        for q in (2, 1, 3):
+            gathers[r, 3 + q] = zcopy(mwbuf.at[r, 0], mwbuf.at[r, 4 - q], q, r, 10 + q)
         gathers[r, 3] = zcopy(vbuf.at[r, 0], vbuf.at[r, 3], 1, r, 9)
         gathers[r, 1] = zcopy(vbuf.at[r, 0], vbuf.at[r, 1], 3, r, 10)
-        for q in (1, 2, 3):
-            gathers[r, 3 + q] = zcopy(mwbuf.at[r, 0], mwbuf.at[r, 4 - q], q, r, 10 + q)
 
     def pass_on(r):
         gathers[r, 3].wait_recv()
         forward[r, 0] = zcopy(vbuf.at[r, 3, 0], vbuf.at[r, 2, 0], 1, r, 14)
         gathers[r, 1].wait_recv()
         forward[r, 1] = zcopy(vbuf.at[r, 1, 1], vbuf.at[r, 2, 1], 3, r, 15)
-        for q in (1, 2, 3):
-            gathers[r, 3 + q].wait_recv()
+        gathers[r, 4].wait_recv()
+        gathers[r, 6].wait_recv()
 
     def perturb():
         bg_load.wait()
@@ -343,19 +345,32 @@
     for q in (2, 1, 3):
         gram(0, q)
         if q == 2:
-            pl.semaphore_wait(barrier, GRP - 1 + 3)
+            pl.semaphore_wait(barrier, 8)
+            tell(known.at[0], SIDE_X)
         send_parts(0, q)
+        if q == 2:
+            loads[0, 0].start()
+            for p in (2, 1, 3, 0):
+                loads[1, p].start()
+            bg_load.start()
+    pl.semaphore_wait(known.at[0], 2)
+    tell(known.at[1], SIDE_Y)
     gram(0, 0)
     for q in (2, 1, 3, 0):
         gram(1, q)
     combine(0)
     for q in (2, 1, 3):
         send_parts(1, q)
+    pl.semaphore_wait(known.at[1], 2)
+    tell(known.at[2], SIDE_Y)
     perturb()
     index()
+    pl.semaphore_wait(known.at[2], 2)
+    tell(known.at[3], CORE)
     newton(0)
     combine(1)
     gather(0)
+    pl.semaphore_wait(known.at[3], 1)
     apply(0, 0)
     newton(1)
     gather(1)
@@ -367,6 +382,7 @@
     apply(1, 1)
     apply(1, 3)
     for r in range(ROUNDS):
+        gathers[r, 5].wait_recv()
         forward[r, 0].wait_recv()
         forward[r, 1].wait_recv()
         apply(r, 2)
@@ -471,6 +487,7 @@
             pltpu.SemaphoreType.DMA((9, 32)),
             pltpu.SemaphoreType.DMA((9,)),
             pltpu.SemaphoreType.DMA((5,)),
+            pltpu.SemaphoreType.REGULAR((4,)),
         ],
         compiler_params=pltpu.CompilerParams(
             collective_id=0, has_side_effects=True, vmem_limit_bytes=44 * 1024 * 1024

time: 88.3 us -> 86.1 us (0.975)
  Pallas kernels: 86.6 us -> 84.7 us
    pallas_call x1, Pallas kernels: 86.6 us -> 84.7 us  [analyse(): pl.pallas_call(kernel, out_shape=jax.ShapeDtypeStruct(background.shape, B...]
where the time goes in v5:
time: 86.1 us; the launch traced here: 86 us
  Pallas kernels  84.7 us (98%)
  local copies, waits for them, and re-layouts  1.32 us (2%)
    pallas_call x1, Pallas kernels, analyse(): pl.pallas_call(kernel, out_shape=jax.ShapeDtypeStruct(background.shape, B...  84.7 us

profile of v5, /device:TPU:1, one launch (start us, length us, event | category | flops | bytes accessed | tf_op | source)
XLA Modules:
  0.0 86.0 jit_solution(16541904334174393047)
XLA Ops:
  0.0 84.7 %shard_map.64 = bf16[8,256,512]{2,1,0:T(8,128)(2,1)S(1)} custom-call(s32[1,256]{1,0:T(1,128)} %bitcast.2, bf16[8,512,512]{2,1,0:T(8,128)(2,1)} %obs_hbm.1, bf16[8,256,512]{2,1,0:T(8,128)(2,1)} %bg_hbm.1, bf16[8,512]{1,0:T(8,128)(2,1)} %innov_hbm.1, bf16[8,512]{1,0:T(8,128)(2,1)} %weight_hbm.1, s32[1,8]{1,0:T(1,128)} %bitcast.3), custom_call_target="tpu_custom_call" | custom-call | tf_op jit(solution)/shard_map/pallas_call | solution.py:448
  84.7 1.3 %copy.8 = bf16[8,256,512]{2,1,0:T(8,128)(2,1)} copy(bf16[8,256,512]{2,1,0:T(8,128)(2,1)S(1)} %shard_map.64) | data formatting | bytes 4194304

commit v6 on v5

--- a/solution.py
+++ b/solution.py
@@ -331,7 +331,7 @@
                 spread[e, h * 16 + k] = block[k * 16 : (k + 1) * 16]
 
         def launch(i, carry):
-            spread_copy(e, step(i)).start()
+            spread_copy(e, step(i + 7 * e)).start()
             return carry
 
         lax.fori_loop(0, GRP - 1, launch, 0)

time: 86.1 us -> 86.1 us (level)
  no operation moved by 1% of the time
where the time goes in v6:
time: 86.1 us; the launch traced here: 86 us
  Pallas kernels  84.7 us (98%)
  local copies, waits for them, and re-layouts  1.32 us (2%)
    pallas_call x1, Pallas kernels, analyse(): pl.pallas_call(kernel, out_shape=jax.ShapeDtypeStruct(background.shape, B...  84.7 us

profile of v6, /device:TPU:1, one launch (start us, length us, event | category | flops | bytes accessed | tf_op | source)
XLA Modules:
  0.0 86.0 jit_solution(11178589193087999266)
XLA Ops:
  0.0 84.7 %shard_map.64 = bf16[8,256,512]{2,1,0:T(8,128)(2,1)S(1)} custom-call(s32[1,256]{1,0:T(1,128)} %bitcast.2, bf16[8,512,512]{2,1,0:T(8,128)(2,1)} %obs_hbm.1, bf16[8,256,512]{2,1,0:T(8,128)(2,1)} %bg_hbm.1, bf16[8,512]{1,0:T(8,128)(2,1)} %innov_hbm.1, bf16[8,512]{1,0:T(8,128)(2,1)} %weight_hbm.1, s32[1,8]{1,0:T(1,128)} %bitcast.3), custom_call_target="tpu_custom_call" | custom-call | tf_op jit(solution)/shard_map/pallas_call | solution.py:448
  84.7 1.3 %copy.8 = bf16[8,256,512]{2,1,0:T(8,128)(2,1)} copy(bf16[8,256,512]{2,1,0:T(8,128)(2,1)S(1)} %shard_map.64) | data formatting | bytes 4194304
